TPU v7x, 32 devices: a whole 2x2x4 slice. The times are simulated.
32 devices in a mesh: dp: 8 (over z, x), rows: 4 (over y, core).
Axes of the slice: x: 2, y: 2, z: 4, core: 2. Of those that a mesh axis runs over, the one named last changes fastest.
Arguments:
- clean: bfloat16 [8, 32, 16, 640], P('dp', 'rows'), may hold values from -6 to 6
- noise: bfloat16 [8, 32, 16, 640], P('dp', 'rows'), may hold values from -6 to 6
- heights: int32 [8], P('dp'), may hold values from 8 to 32, as said below
- widths: int32 [8], P('dp'), may hold values from 4 to 16, as said below
- levels: int32 [8], P('dp'), may hold values from 0 to 8
- gain: float32 [640], replicated, may hold values from 0.25 to 1.75
- shift: float32 [640], replicated, may hold values from -3 to 3
- emb_table: float32 [10, 640], replicated, may hold values from -5 to 5
- w_student: bfloat16 [640, 3, 3, 640], P('dp'), may hold values from -0.078125 to 0.078125
- w_ema: bfloat16 [640, 3, 3, 640], P('dp'), may hold values from -0.078125 to 0.078125
Outputs:
- grad_conv: float32 [640, 3, 3, 640], P('dp')
- grad_gain: float32 [640], replicated
- grad_shift: float32 [640], replicated
- loss: float32 [], replicated
Inputs may be any that keep to these rules, and one draw needn't show every extreme that they name: Each sample's valid rows are its first heights rows; at least one sample covers all 32 rows. Each sample's valid columns are its first widths columns; at least one sample covers all 16 columns.
All inputs are finite; a program needn't handle non-finite values.
Results may differ from a plain program's by a relative error of at most 0.00064.
Values may be sent and summed in bfloat16 or wider, within the bound.
No kernel may reach another device: no remote copies, remote signals or barrier semaphores. Data moves between devices by JAX's collectives and lax.ppermute only.
A program may use at most 128 MiB of HBM per device.

v0:
```python
import jax
import jax.numpy as jnp
from jax import lax
from jax.sharding import PartitionSpec as P

C = 640
GROUPS = 32
NSTEPS = 10
SAMP_DEV = 1
ROWS_DEV = 8
WID = 16
SIGMA_DATA = 0.5
SIGMA_FLOOR = 0.002
SIGMA_CEIL = 80.0


def padded_2(block, sides, width):
    for axis, dim in sides:
        count = lax.axis_size(axis)
        forward = [(i, i + 1) for i in range(count - 1)]
        backward = [(target, source) for source, target in forward]
        low = lax.ppermute(
            lax.slice_in_dim(block, block.shape[dim] - width, None, axis=dim), axis, forward
        )
        high = lax.ppermute(lax.slice_in_dim(block, 0, width, axis=dim), axis, backward)
        block = jnp.concatenate([low, block, high], axis=dim)
    return block


def sigma_table():
    ladder = jnp.arange(NSTEPS, dtype=jnp.float32) / (NSTEPS - 1)
    lowest = SIGMA_FLOOR ** (1.0 / 7.0)
    highest = SIGMA_CEIL ** (1.0 / 7.0)
    return (lowest + ladder * (highest - lowest)) ** 7


def scale_factors(noise_stddev):
    input_scale = 1.0 / jnp.sqrt(noise_stddev * noise_stddev + SIGMA_DATA**2)
    lifted = noise_stddev - SIGMA_FLOOR
    bypass_scale = SIGMA_DATA**2 / (lifted * lifted + SIGMA_DATA**2)
    output_scale = SIGMA_DATA * lifted / jnp.sqrt(SIGMA_DATA**2 + noise_stddev * noise_stddev)
    return (input_scale, bypass_scale, output_scale)


def silu_slope(value):
    sigmoid_value = jax.nn.sigmoid(value)
    return sigmoid_value * (1.0 + value * (1.0 - sigmoid_value))


def pad_active(active):
    framed = padded_2(active, (("rows", 1),), 1)
    return jnp.pad(framed, ((0, 0), (0, 0), (1, 1), (0, 0)))


def pad_gradient(grad_out):
    framed = padded_2(grad_out, (("rows", 1),), 1)
    return jnp.pad(framed, ((0, 0), (0, 0), (1, 1), (0, 0)))


def conv_full(padded, weights):
    result = jnp.zeros((SAMP_DEV, ROWS_DEV, WID, C), jnp.float32)
    for tap_row in range(3):
        for tap_col in range(3):
            window = padded[:, tap_row : tap_row + ROWS_DEV, tap_col : tap_col + WID, :]
            result = result + jnp.einsum(
                "srwc,cd->srwd",
                window,
                weights[:, tap_row, tap_col, :],
                preferred_element_type=jnp.float32,
            )
    return result


def stacked_term(routed, collected):
    owned_width = routed.shape[3]
    windows = []
    for tap_row in range(3):
        for tap_col in range(3):
            windows.append(routed[:, tap_row : tap_row + ROWS_DEV, tap_col : tap_col + WID, :])
    stacked = jnp.concatenate(windows, axis=3)
    product = jnp.einsum("srwk,srwd->kd", stacked, collected, preferred_element_type=jnp.float32)
    return product.reshape(3, 3, owned_width, C).transpose(2, 0, 1, 3)


def group_norm(inner, valid, count):
    grouped = inner.reshape(SAMP_DEV, ROWS_DEV, WID, GROUPS, C // GROUPS)
    weight_mask = valid[..., None]
    denom = (count * (C // GROUPS))[:, None]
    first = lax.psum(jnp.sum(weight_mask * grouped, axis=(1, 2, 4)), "rows")
    center = first / denom
    offset = grouped - center[:, None, None, :, None]
    spread = lax.psum(jnp.sum(weight_mask * offset * offset, axis=(1, 2, 4)), "rows") / denom
    normed = (grouped - center[:, None, None, :, None]) / jnp.sqrt(
        spread[:, None, None, :, None] + 1e-05
    )
    return normed.reshape(SAMP_DEV, ROWS_DEV, WID, C)


def forward(clean, noise, valid, count, noise_stddev, embed, gain, shift, weights):
    input_scale, bypass_scale, output_scale = scale_factors(noise_stddev[:, None, None, None])
    noisy = clean.astype(jnp.float32) + noise_stddev[:, None, None, None] * noise.astype(
        jnp.float32
    )
    inner = input_scale * noisy + embed[:, None, None, :]
    normed = group_norm(inner, valid, count)
    preact = normed * gain + shift
    active = (valid * jax.nn.silu(preact)).astype(jnp.bfloat16)
    padded = pad_active(active)
    conv_out = conv_full(padded, weights)
    output = bypass_scale * noisy + output_scale * (input_scale * noisy + conv_out)
    return (output, padded, normed, preact)


def shards(clean, noise, heights, widths, levels, gain, shift, emb_table, w_student, w_ema):
    noise_stddevs = sigma_table()
    level_ids = jnp.arange(NSTEPS, dtype=jnp.int32)[None, :]
    lower_hot = (levels[:, None] == level_ids).astype(jnp.float32)
    upper_hot = ((levels + 1)[:, None] == level_ids).astype(jnp.float32)
    sigma_target = jnp.sum(lower_hot * noise_stddevs[None, :], axis=1)
    student_stddev = jnp.sum(upper_hot * noise_stddevs[None, :], axis=1)
    embed_target = jnp.sum(lower_hot[:, :, None] * emb_table[None], axis=1)
    embed_student = jnp.sum(upper_hot[:, :, None] * emb_table[None], axis=1)
    row_start = lax.axis_index("rows") * ROWS_DEV
    rows_at = row_start + jnp.arange(ROWS_DEV, dtype=jnp.int32)
    cols_at = jnp.arange(WID, dtype=jnp.int32)
    valid = (rows_at[None, :, None] < heights[:, None, None]) & (
        cols_at[None, None, :] < widths[:, None, None]
    )
    valid = valid.astype(jnp.float32)[..., None]
    count = (heights * widths).astype(jnp.float32)
    student_full, target_full = (
        lax.all_gather(w_student, "dp", axis=0, tiled=True),
        lax.all_gather(w_ema, "dp", axis=0, tiled=True),
    )
    target, _, _, _ = forward(
        clean, noise, valid, count, sigma_target, embed_target, gain, shift, target_full
    )
    student, padded, normed, preact = forward(
        clean, noise, valid, count, student_stddev, embed_student, gain, shift, student_full
    )
    delta = valid * (student - target)
    loss_local = jnp.sum(jnp.sum(delta * delta, axis=(1, 2, 3)) / count)
    output_scale = scale_factors(student_stddev)[2]
    grad_out = ((2.0 * output_scale / count)[:, None, None, None] * delta).astype(jnp.bfloat16)
    routed = lax.all_to_all(padded, "dp", split_axis=3, concat_axis=0, tiled=True)
    collected = lax.all_gather(grad_out, "dp", axis=0, tiled=True)
    owned = stacked_term(routed, collected)
    grad_conv = lax.psum(owned, "rows")
    grad_pad = pad_gradient(grad_out)
    back = jnp.zeros((SAMP_DEV, ROWS_DEV, WID, C), jnp.float32)
    for tap_row in range(3):
        for tap_col in range(3):
            window = grad_pad[
                :, 2 - tap_row : 2 - tap_row + ROWS_DEV, 2 - tap_col : 2 - tap_col + WID, :
            ]
            back = back + jnp.einsum(
                "srwd,cd->srwc",
                window,
                student_full[:, tap_row, tap_col, :],
                preferred_element_type=jnp.float32,
            )
    grad_pre = back * valid * silu_slope(preact)
    gain_local = jnp.sum(grad_pre * normed, axis=(0, 1, 2))
    shift_local = jnp.sum(grad_pre, axis=(0, 1, 2))
    grad_gain, grad_shift, loss_total = lax.psum(
        (gain_local, shift_local, loss_local), ("dp", "rows")
    )
    loss = loss_total / (SAMP_DEV * lax.axis_size("dp") * C)
    return (grad_conv, grad_gain, grad_shift, loss)


def solution(mesh):
    placed = (
        P("dp", "rows", None, None),
        P("dp", "rows", None, None),
        P("dp"),
        P("dp"),
        P("dp"),
        P(),
        P(),
        P(),
        P("dp", None, None, None),
        P("dp", None, None, None),
    )
    return jax.shard_map(
        shards,
        mesh=mesh,
        in_specs=placed,
        out_specs=(P("dp", None, None, None), P(), P(), P()),
        check_vma=False,
    )
```

profile of v0, /device:TPU:0, one launch (start us, length us, event | category | flops | bytes accessed | tf_op | source)
XLA Modules:
  0.0 362.8 jit_solution(16485923307652511653)
XLA Ops:
  14.8 2.4 multiply_reduce_fusion.2
  17.6 8.4 %all-reduce.5 = (f32[1,32]{1,0:T(1,128)S(1)}, f32[1,32]{1,0:T(1,128)S(1)}) all-reduce(f32[1,32]{1,0:T(1,128)S(1)} %bitcast.263, f32[1,32]{1,0:T(1,128)S(1)} %bitcast.261), channel_id=1, replica_groups=mesh['dp'=8,'rows'=4] {'rows'}, use_global_device_ids=true, to_apply=%region_12.13 | all-reduce | flops 64 | bytes 512 | tf_op jit(solution)/shard_map/psum | solution.py:89
  26.4 2.4 fusion.25
  29.2 6.1 %all-reduce.4 = (f32[1,32]{1,0:T(1,128)S(1)}, f32[1,32]{1,0:T(1,128)S(1)}) all-reduce(f32[1,32]{1,0:T(1,128)S(1)} %bitcast.264, f32[1,32]{1,0:T(1,128)S(1)} %bitcast.262), channel_id=1, replica_groups=mesh['dp'=8,'rows'=4] {'rows'}, use_global_device_ids=true, to_apply=%region_7.0 | all-reduce | flops 64 | bytes 512 | tf_op jit(solution)/shard_map/psum | solution.py:92
  35.7 2.6 multiply_convert_fusion.1
  41.0 3.6 collective-permute-start.2
  47.5 2.3 copy.20
  49.8 2.8 reshape.527
  52.6 6.1 %all-to-all-start = ((bf16[8,2,7200]{2,1,0:T(2,128)(2,1)}), bf16[8,2,7200]{2,1,0:T(2,128)(2,1)}, u32[]{:S(2)}, u32[]{:S(2)}) async-start(bf16[8,2,7200]{2,1,0:T(2,128)(2,1)} %reshape.527), calls=%async_computation | async-start | bytes 466944 | tf_op jit(solution)/shard_map/all_to_all | solution.py:145
  59.6 68.1 %all-gather.4.cloned.1.call-done = bf16[640,3,3,640]{3,0,2,1:T(8,128)(2,1)} async-done(((bf16[80,3,3,640]{3,0,2,1:T(8,128)(2,1)}), bf16[640,3,3,640]{3,0,2,1:T(8,128)(2,1)}) %all-gather.4.cloned.1.call-update) | async-done | bytes 7372816 | tf_op jit(solution)/shard_map/all_gather | solution.py:132
  127.7 2.3 fusion.20
  130.0 2.2 fusion.22
  132.2 108.7 %all-gather.6.cloned.1.call-done = bf16[640,3,3,640]{3,0,2,1:T(8,128)(2,1)} async-done(((bf16[80,3,3,640]{3,0,2,1:T(8,128)(2,1)}), bf16[640,3,3,640]{3,0,2,1:T(8,128)(2,1)}) %all-gather.6.cloned.1.call-update) | async-done | bytes 7372816 | tf_op jit(solution)/shard_map/all_gather | solution.py:133
  240.9 1.6 fusion.18
  245.7 1.7 convolution_add_fusion.12
  256.5 3.4 multiply_reduce_fusion
  259.9 3.3 reshape.528
  263.2 2.0 copy.22
  269.9 2.8 concatenate.31
  281.1 18.8 %all-gather.8.cloned.1.call-done = bf16[8,8,16,640]{3,2,1,0:T(8,128)(2,1)} async-done(((bf16[1,8,16,640]{3,2,1,0:T(8,128)(2,1)}), bf16[8,8,16,640]{3,2,1,0:T(8,128)(2,1)}) %all-gather.8.cloned.1.call-update) | async-done | bytes 1310736 | tf_op jit(solution)/shard_map/all_gather | solution.py:146
  299.9 3.9 %fusion = f32[720,640,1,1]{1,0,3,2:T(8,128)} fusion(bf16[8,8,16,720]{3,2,0,1:T(8,128)(2,1)S(1)} %concatenate.31, bf16[8,8,16,640]{3,2,1,0:T(8,128)(2,1)} %all-gather.8.cloned.1.call-done), kind=kOutput, calls=%fused_computation | convolution fusion | flops 943718400 | bytes 4628480 | tf_op jit(solution)/shard_map/srwk,srwd->kd/dot_general | solution.py:81
  308.5 2.3 fusion.57
  310.7 40.8 %all-reduce.3 = (f32[640]{0:T(1024)}, f32[640]{0:T(1024)}, f32[]{:T(128)}) all-reduce(f32[640]{0:T(1024)S(1)} %get-tuple-element.9, f32[640]{0:T(1024)S(1)} %get-tuple-element.8, f32[]{:T(128)} %bitcast.99), channel_id=1, replica_groups=mesh['dp'=8,'rows'=4] {'dp','rows'}, use_global_device_ids=true, to_apply=%region_18.19 | all-reduce | flops 1281 | bytes 10248 | tf_op jit(solution)/shard_map/psum | solution.py:165
  352.3 2.9 copy.33
  (120 shorter events, 38.6 us)
Async XLA Ops:
  7.2 120.5 %all-gather.4.cloned.1.call-start = ((), (), s32[]{:S(2)}) async-start(), calls=%async_computation.1 | async-start | bytes 8294400 | tf_op jit(solution)/shard_map/all_gather | solution.py:132
  7.9 233.0 %all-gather.6.cloned.1.call-start = ((), (), s32[]{:S(2)}) async-start(), calls=%async_computation.2 | async-start | bytes 8294400 | tf_op jit(solution)/shard_map/all_gather | solution.py:133
  26.2 33.4 %copy-start.12 = (f32[640]{0:T(1024)}, f32[640]{0:T(1024)S(1)}, u32[]{:S(2)}) copy-start(f32[640]{0:T(1024)S(1)} %sub.69) | copy-start | bytes 7684
  38.3 21.3 %copy-start.3 = (bf16[1,8,16,640]{3,2,1,0:T(8,128)(2,1)}, bf16[1,8,16,640]{3,2,1,0:T(8,128)(2,1)S(1)}, u32[]{:S(2)}) copy-start(bf16[1,8,16,640]{3,2,1,0:T(8,128)(2,1)S(1)} %get-tuple-element.28) | copy-start | bytes 491524
  38.3 9.0 %collective-permute-start = (bf16[1,1,16,640]{3,2,1,0:T(8,128)(2,1)S(1)}, bf16[1,1,16,640]{3,2,1,0:T(8,128)(2,1)S(1)}, u32[]{:S(2)}, u32[]{:S(2)}) collective-permute-start(bf16[1,1,16,640]{3,2,1,0:T(8,128)(2,1)S(1)} %get-tuple-element.36), channel_id=1, source_target_pairs={{0,1},{1,2},{2,3},{4,5},{5,6},{6,7},{8,9},{9,10},{10,11},{12,13},{... | collective-permute-start | bytes 61448 | tf_op jit(solution)/shard_map/ppermute | solution.py:22
  39.7 7.6 %collective-permute-start.1 = (bf16[1,1,16,640]{3,2,1,0:T(8,128)(2,1)S(1)}, bf16[1,1,16,640]{3,2,1,0:T(8,128)(2,1)S(1)}, u32[]{:S(2)}, u32[]{:S(2)}) collective-permute-start(bf16[1,1,16,640]{3,2,1,0:T(8,128)(2,1)S(1)} %get-tuple-element.37), channel_id=1, source_target_pairs={{1,0},{2,1},{3,2},{5,4},{6,5},{7,6},{9,8},{10,9},{11,10},{13,12},{... | collective-permute-start | bytes 61448 | tf_op jit(solution)/shard_map/ppermute | solution.py:25
  41.0 17.7 %collective-permute-start.2 = (bf16[1,1,16,640]{3,2,1,0:T(8,128)(2,1)S(1)}, bf16[1,1,16,640]{3,2,1,0:T(8,128)(2,1)S(1)}, u32[]{:S(2)}, u32[]{:S(2)}) collective-permute-start(bf16[1,1,16,640]{3,2,1,0:T(8,128)(2,1)S(1)} %get-tuple-element.34), channel_id=1, source_target_pairs={{0,1},{1,2},{2,3},{4,5},{5,6},{6,7},{8,9},{9,10},{10,11},{12,13},{... | collective-permute-start | bytes 61448 | tf_op jit(solution)/shard_map/ppermute | solution.py:22
  44.6 14.2 %collective-permute-start.3 = (bf16[1,1,16,640]{3,2,1,0:T(8,128)(2,1)S(1)}, bf16[1,1,16,640]{3,2,1,0:T(8,128)(2,1)S(1)}, u32[]{:S(2)}, u32[]{:S(2)}) collective-permute-start(bf16[1,1,16,640]{3,2,1,0:T(8,128)(2,1)S(1)} %get-tuple-element.35), channel_id=1, source_target_pairs={{1,0},{2,1},{3,2},{5,4},{6,5},{7,6},{9,8},{10,9},{11,10},{13,12},{... | collective-permute-start | bytes 61448 | tf_op jit(solution)/shard_map/ppermute | solution.py:25
  52.6 207.3 %all-to-all-start = ((bf16[8,2,7200]{2,1,0:T(2,128)(2,1)}), bf16[8,2,7200]{2,1,0:T(2,128)(2,1)}, u32[]{:S(2)}, u32[]{:S(2)}) async-start(bf16[8,2,7200]{2,1,0:T(2,128)(2,1)} %reshape.527), calls=%async_computation | async-start | bytes 466944 | tf_op jit(solution)/shard_map/all_to_all | solution.py:145
  58.7 241.2 %all-gather.8.cloned.1.call-start = ((), (), s32[]{:S(2)}) async-start(), calls=%async_computation.3 | async-start | bytes 1474560 | tf_op jit(solution)/shard_map/all_gather | solution.py:146
  127.7 125.8 %slice-start = ((s8[7372800]{0:T(1024)(128)(4,1)}), s8[3178496]{0:T(1024)(128)(4,1)S(1)}, s32[]{:S(2)}) async-start(s8[7372800]{0:T(1024)(128)(4,1)} %bitcast.255), calls=%async_computation.5 | async-start | bytes 6356992
  240.9 9.7 %copy-start.2 = (bf16[1,10,18,640]{3,2,1,0:T(8,128)(2,1)S(1)}, bf16[1,10,18,640]{3,2,1,0:T(8,128)(2,1)}, u32[]{:S(2)}) copy-start(bf16[1,10,18,640]{3,2,1,0:T(8,128)(2,1)} %select_maximum_fusion.2) | copy-start | bytes 691204
  240.9 12.6 %copy-start.1 = (bf16[1,8,16,640]{3,2,1,0:T(8,128)(2,1)S(1)}, bf16[1,8,16,640]{3,2,1,0:T(8,128)(2,1)}, u32[]{:S(2)}) copy-start(bf16[1,8,16,640]{3,2,1,0:T(8,128)(2,1)} %copy-done) | copy-start | bytes 491524
  240.9 12.6 %copy-start.10 = (f32[8,16,640]{2,1,0:T(8,128)S(1)}, f32[8,16,640]{2,1,0:T(8,128)}, u32[]{:S(2)}) copy-start(f32[8,16,640]{2,1,0:T(8,128)} %fusion.20) | copy-start | bytes 983044
  259.9 13.5 %copy-start.5 = (bf16[1,8,16,640]{3,2,1,0:T(8,128)(2,1)S(1)}, bf16[1,8,16,640]{3,2,1,0:T(8,128)(2,1)}, u32[]{:S(2)}) copy-start(bf16[1,8,16,640]{3,2,1,0:T(8,128)(2,1)} %get-tuple-element.31) | copy-start | bytes 491524
  259.9 92.4 %all-reduce.8.cloned.1.call-start = ((), (), s32[]{:S(2)}) async-start(), calls=%async_computation.4 | async-start | bytes 3686400 | tf_op jit(solution)/shard_map/psum | solution.py:148
  265.9 7.3 %collective-permute-start.4 = (bf16[1,1,16,640]{3,2,1,0:T(8,128)(2,1)S(1)}, bf16[1,1,16,640]{3,2,1,0:T(8,128)(2,1)S(1)}, u32[]{:S(2)}, u32[]{:S(2)}) collective-permute-start(bf16[1,1,16,640]{3,2,1,0:T(8,128)(2,1)S(1)} %get-tuple-element.32), channel_id=1, source_target_pairs={{0,1},{1,2},{2,3},{4,5},{5,6},{6,7},{8,9},{9,10},{10,11},{12,13},{... | collective-permute-start | bytes 61448 | tf_op jit(solution)/shard_map/ppermute | solution.py:22
  267.2 6.1 %collective-permute-start.5 = (bf16[1,1,16,640]{3,2,1,0:T(8,128)(2,1)S(1)}, bf16[1,1,16,640]{3,2,1,0:T(8,128)(2,1)S(1)}, u32[]{:S(2)}, u32[]{:S(2)}) collective-permute-start(bf16[1,1,16,640]{3,2,1,0:T(8,128)(2,1)S(1)} %get-tuple-element.33), channel_id=1, source_target_pairs={{1,0},{2,1},{3,2},{5,4},{6,5},{7,6},{9,8},{10,9},{11,10},{13,12},{... | collective-permute-start | bytes 61448 | tf_op jit(solution)/shard_map/ppermute | solution.py:25
  281.0 27.4 %copy-start.7 = (bf16[1,8,16,640]{3,2,1,0:T(8,128)(2,1)S(1)}, bf16[1,8,16,640]{3,2,1,0:T(8,128)(2,1)}, u32[]{:S(2)}) copy-start(bf16[1,8,16,640]{3,2,1,0:T(8,128)(2,1)} %param.11) | copy-start | bytes 491524
  281.0 27.4 %copy-start.9 = (bf16[1,8,16,640]{3,2,1,0:T(8,128)(2,1)S(1)}, bf16[1,8,16,640]{3,2,1,0:T(8,128)(2,1)}, u32[]{:S(2)}) copy-start(bf16[1,8,16,640]{3,2,1,0:T(8,128)(2,1)} %param.10) | copy-start | bytes 491524
  281.0 27.4 %copy-start.13 = (f32[640]{0:T(1024)S(1)}, f32[640]{0:T(1024)}, u32[]{:S(2)}) copy-start(f32[640]{0:T(1024)} %copy-done.12) | copy-start | bytes 7684
  281.1 27.4 %copy-start.17 = (f32[640]{0:T(1024)S(1)}, f32[640]{0:T(1024)}, u32[]{:S(2)}) copy-start(f32[640]{0:T(1024)} %copy-done.16) | copy-start | bytes 7684
  281.1 27.4 %copy-start.18 = (f32[640]{0:T(1024)S(1)}, f32[640]{0:T(1024)}, u32[]{:S(2)}) copy-start(f32[640]{0:T(1024)} %param.16) | copy-start | bytes 7684
  281.1 27.4 %copy-start.19 = (f32[640]{0:T(1024)S(1)}, f32[640]{0:T(1024)}, u32[]{:S(2)}) copy-start(f32[640]{0:T(1024)} %param.15) | copy-start | bytes 7684
  (9 other events, 56.6 us)
Sparse Core Ops, SparseCore 0:
  10.2 117.3 all-gather.3
  129.9 110.9 all-gather.5
  260.0 39.9 all-gather.7
  304.0 47.7 all-reduce.7
where the time goes:
time: 364 us; the launch traced here: 363 us
  waiting for transfers between devices  197 us (54%)
  blocking collectives  55.3 us (15%)
  matrix products  41.4 us (11%)
  between operations  22.9 us (6%)
  local copies, waits for them, and re-layouts  19.1 us (5%)
  starting transfers between devices  16.5 us (5%)
  other arithmetic  10.5 us (3%)
    all_gather x1, waiting for transfers between devices, shards(): lax.all_gather(w_ema, 'dp', axis=0, tiled=True)  109 us
    all_gather x1, waiting for transfers between devices, shards(): lax.all_gather(w_student, 'dp', axis=0, tiled=True)  68.1 us
    psum x1, blocking collectives, shards(): lax.psum((gain_local, shift_local, loss_local), ('dp', 'rows'))  40.8 us
    dot_general x18, matrix products, conv_full(): jnp.einsum('srwc,cd->srwd', window, weights[:, tap_row, tap_col, :], pref...  23.2 us
    all_gather x1, waiting for transfers between devices, shards(): collected = lax.all_gather(grad_out, 'dp', axis=0, tiled=True)  18.8 us
    dot_general x9, matrix products, shards(): jnp.einsum('srwd,cd->srwc', window, student_full[:, tap_row, tap_col, :],...  14.3 us
    unnamed x47, local copies, waits for them, and re-layouts  9.06 us
    psum x1, blocking collectives, group_norm(): first = lax.psum(jnp.sum(weight_mask * grouped, axis=(1, 2, 4)), 'rows')  8.4 us
  transfers between devices with their start and end apart: 11, of which 3 were waited for; matrix products, arithmetic and copies ran while one was open for 18% of the time, Pallas kernels for 0%

commit v1 on v0

--- a/solution.py
+++ b/solution.py
@@ -1,3 +1,4 @@
+import functools
 import jax
 import jax.numpy as jnp
 from jax import lax
@@ -12,6 +13,26 @@
 SIGMA_DATA = 0.5
 SIGMA_FLOOR = 0.002
 SIGMA_CEIL = 80.0
+
+
+def feed_samples_all(array_here, axis_name):
+    axis_total = lax.axis_size(axis_name)
+    items = []
+    for nth in tuple(range(axis_total)):
+        items.append((nth, (nth + 1) % axis_total))
+
+    def define_notes(even):
+        if len(even) == axis_total:
+            return even
+        return define_notes([lax.ppermute(even[0], axis_name, items), *even])
+
+    field_out = define_notes([array_here])
+    long_array = jnp.concatenate(field_out, 0)
+    e_next = lax.axis_index(axis_name)
+    return jnp.roll(long_array, (e_next + 1) * array_here.shape[0], 0)
+
+
+convert_run = functools.partial(feed_samples_all, axis_name="dp")
 
 
 def padded_2(block, sides, width):
@@ -143,7 +164,7 @@
     output_scale = scale_factors(student_stddev)[2]
     grad_out = ((2.0 * output_scale / count)[:, None, None, None] * delta).astype(jnp.bfloat16)
     routed = lax.all_to_all(padded, "dp", split_axis=3, concat_axis=0, tiled=True)
-    collected = lax.all_gather(grad_out, "dp", axis=0, tiled=True)
+    collected = convert_run(grad_out)
     owned = stacked_term(routed, collected)
     grad_conv = lax.psum(owned, "rows")
     grad_pad = pad_gradient(grad_out)

time: 364 us -> 379 us (1.041)
  waiting for transfers between devices: 197 us -> 212 us
    ppermute x0 -> x7, waiting for transfers between devices: none -> 41.7 us  [define_notes(): return define_notes([lax.ppermute(even[0], axis_name, items), *even])]
    all_gather x1 -> x0, waiting for transfers between devices: 18.8 us -> none  [shards(): collected = lax.all_gather(grad_out, 'dp', axis=0, tiled=True)]
    all_gather x1, waiting for transfers between devices: 68.1 us -> 58.2 us  [shards(): lax.all_gather(w_student, 'dp', axis=0, tiled=True)]
    unnamed x47 -> x74, local copies, waits for them, and re-layouts: 9.06 us -> 10.9 us
  transfers between devices with their start and end apart: 11 -> 17, of which waited for: 3 -> 12; matrix products, arithmetic and copies ran while one was open for 18% -> 12% of each run, Pallas kernels for 0% -> 0%
where the time goes in v1:
time: 379 us; the launch traced here: 377 us
  waiting for transfers between devices  212 us (56%)
  blocking collectives  53.2 us (14%)
  matrix products  39.3 us (10%)
  between operations  23 us (6%)
  local copies, waits for them, and re-layouts  21.2 us (6%)
  starting transfers between devices  17.9 us (5%)
  other arithmetic  10.2 us (3%)
    all_gather x1, waiting for transfers between devices, shards(): lax.all_gather(w_ema, 'dp', axis=0, tiled=True)  108 us
    all_gather x1, waiting for transfers between devices, shards(): lax.all_gather(w_student, 'dp', axis=0, tiled=True)  58.2 us
    ppermute x7, waiting for transfers between devices, define_notes(): return define_notes([lax.ppermute(even[0], axis_name, items), *even])  41.7 us
    psum x1, blocking collectives, shards(): lax.psum((gain_local, shift_local, loss_local), ('dp', 'rows'))  38.8 us
    dot_general x18, matrix products, conv_full(): jnp.einsum('srwc,cd->srwd', window, weights[:, tap_row, tap_col, :], pref...  22.2 us
    dot_general x9, matrix products, shards(): jnp.einsum('srwd,cd->srwc', window, student_full[:, tap_row, tap_col, :],...  14.5 us
    unnamed x74, local copies, waits for them, and re-layouts  10.9 us
    psum x1, blocking collectives, group_norm(): first = lax.psum(jnp.sum(weight_mask * grouped, axis=(1, 2, 4)), 'rows')  8.4 us
  transfers between devices with their start and end apart: 17, of which 12 were waited for; matrix products, arithmetic and copies ran while one was open for 12% of the time, Pallas kernels for 0%

profile of v1, /device:TPU:0, one launch (start us, length us, event | category | flops | bytes accessed | tf_op | source)
XLA Modules:
  0.0 376.8 jit_solution(1888659005624908792)
XLA Ops:
  14.8 2.4 multiply_reduce_fusion.2
  17.6 8.4 %all-reduce.5 = (f32[1,32]{1,0:T(1,128)S(1)}, f32[1,32]{1,0:T(1,128)S(1)}) all-reduce(f32[1,32]{1,0:T(1,128)S(1)} %bitcast.263, f32[1,32]{1,0:T(1,128)S(1)} %bitcast.261), channel_id=1, replica_groups=mesh['dp'=8,'rows'=4] {'rows'}, use_global_device_ids=true, to_apply=%region_12.13 | all-reduce | flops 64 | bytes 512 | tf_op jit(solution)/shard_map/psum | solution.py:110
  26.4 2.4 fusion.25
  29.3 6.1 %all-reduce.4 = (f32[1,32]{1,0:T(1,128)S(1)}, f32[1,32]{1,0:T(1,128)S(1)}) all-reduce(f32[1,32]{1,0:T(1,128)S(1)} %bitcast.264, f32[1,32]{1,0:T(1,128)S(1)} %bitcast.262), channel_id=1, replica_groups=mesh['dp'=8,'rows'=4] {'rows'}, use_global_device_ids=true, to_apply=%region_7.0 | all-reduce | flops 64 | bytes 512 | tf_op jit(solution)/shard_map/psum | solution.py:113
  40.1 2.3 collective-permute-done.1
  44.8 2.8 reshape.527
  47.6 6.1 %all-to-all-start = ((bf16[8,2,7200]{2,1,0:T(2,128)(2,1)}), bf16[8,2,7200]{2,1,0:T(2,128)(2,1)S(1)}, u32[]{:S(2)}, u32[]{:S(2)}) async-start(bf16[8,2,7200]{2,1,0:T(2,128)(2,1)} %reshape.527), calls=%async_computation | async-start | bytes 466944 | tf_op jit(solution)/shard_map/all_to_all | solution.py:166
  53.8 4.5 %collective-permute-start.2 = (bf16[1,1,16,640]{3,2,1,0:T(8,128)(2,1)S(1)}, bf16[1,1,16,640]{3,2,1,0:T(8,128)(2,1)S(1)}, u32[]{:S(2)}, u32[]{:S(2)}) collective-permute-start(bf16[1,1,16,640]{3,2,1,0:T(8,128)(2,1)S(1)} %get-tuple-element.34), channel_id=1, source_target_pairs={{0,1},{1,2},{2,3},{4,5},{5,6},{6,7},{8,9},{9,10},{10,11},{12,13},{... | collective-permute-start | bytes 61448 | tf_op jit(solution)/shard_map/ppermute | solution.py:43
  64.5 2.6 copy.22
  67.1 58.2 %all-gather.3.cloned.1.call-done = bf16[640,3,3,640]{3,0,2,1:T(8,128)(2,1)} async-done(((bf16[80,3,3,640]{3,0,2,1:T(8,128)(2,1)}), bf16[640,3,3,640]{3,0,2,1:T(8,128)(2,1)}) %all-gather.3.cloned.1.call-update) | async-done | bytes 7372816 | tf_op jit(solution)/shard_map/all_gather | solution.py:153
  127.4 2.3 fusion.22
  129.8 107.5 %all-gather.5.cloned.1.call-done = bf16[640,3,3,640]{3,0,2,1:T(8,128)(2,1)} async-done(((bf16[80,3,3,640]{3,0,2,1:T(8,128)(2,1)}), bf16[640,3,3,640]{3,0,2,1:T(8,128)(2,1)}) %all-gather.5.cloned.1.call-update) | async-done | bytes 7372816 | tf_op jit(solution)/shard_map/all_gather | solution.py:154
  252.7 2.7 multiply_reduce_fusion
  259.2 4.3 %collective-permute-done.4 = bf16[1,8,16,640]{3,2,1,0:T(8,128)(2,1)S(1)} collective-permute-done((bf16[1,8,16,640]{3,2,1,0:T(8,128)(2,1)S(1)}, bf16[1,8,16,640]{3,2,1,0:T(8,128)(2,1)S(1)}, u32[]{:S(2)}, u32[]{:S(2)}) %collective-permute-start.4) | collective-permute-done | bytes 163872 | tf_op jit(solution)/shard_map/ppermute | solution.py:27
  264.5 2.6 concatenate.37
  269.2 2.4 collective-permute-done.5
  273.1 6.7 %collective-permute-done.6 = bf16[1,8,16,640]{3,2,1,0:T(8,128)(2,1)S(1)} collective-permute-done((bf16[1,8,16,640]{3,2,1,0:T(8,128)(2,1)}, bf16[1,8,16,640]{3,2,1,0:T(8,128)(2,1)S(1)}, u32[]{:S(2)}, u32[]{:S(2)}) %collective-permute-start.6) | collective-permute-done | bytes 163872 | tf_op jit(solution)/shard_map/ppermute | solution.py:27
  281.3 6.5 %collective-permute-done.7 = bf16[1,8,16,640]{3,2,1,0:T(8,128)(2,1)S(1)} collective-permute-done((bf16[1,8,16,640]{3,2,1,0:T(8,128)(2,1)S(1)}, bf16[1,8,16,640]{3,2,1,0:T(8,128)(2,1)S(1)}, u32[]{:S(2)}, u32[]{:S(2)}) %collective-permute-start.7) | collective-permute-done | bytes 163872 | tf_op jit(solution)/shard_map/ppermute | solution.py:27
  289.3 7.2 %collective-permute-done.8 = bf16[1,8,16,640]{3,2,1,0:T(8,128)(2,1)S(1)} collective-permute-done((bf16[1,8,16,640]{3,2,1,0:T(8,128)(2,1)S(1)}, bf16[1,8,16,640]{3,2,1,0:T(8,128)(2,1)S(1)}, u32[]{:S(2)}, u32[]{:S(2)}) %collective-permute-start.8) | collective-permute-done | bytes 163872 | tf_op jit(solution)/shard_map/ppermute | solution.py:27
  298.0 8.2 %collective-permute-done.9 = bf16[1,8,16,640]{3,2,1,0:T(8,128)(2,1)S(1)} collective-permute-done((bf16[1,8,16,640]{3,2,1,0:T(8,128)(2,1)S(1)}, bf16[1,8,16,640]{3,2,1,0:T(8,128)(2,1)S(1)}, u32[]{:S(2)}, u32[]{:S(2)}) %collective-permute-start.9) | collective-permute-done | bytes 163872 | tf_op jit(solution)/shard_map/ppermute | solution.py:27
  307.7 6.5 %collective-permute-done.10 = bf16[1,8,16,640]{3,2,1,0:T(8,128)(2,1)S(1)} collective-permute-done((bf16[1,8,16,640]{3,2,1,0:T(8,128)(2,1)S(1)}, bf16[1,8,16,640]{3,2,1,0:T(8,128)(2,1)S(1)}, u32[]{:S(2)}, u32[]{:S(2)}) %collective-permute-start.10) | collective-permute-done | bytes 163872 | tf_op jit(solution)/shard_map/ppermute | solution.py:27
  316.5 2.6 fusion
  326.3 38.8 %all-reduce.3 = (f32[640]{0:T(1024)}, f32[640]{0:T(1024)}, f32[]{:T(128)}) all-reduce(f32[640]{0:T(1024)S(1)} %get-tuple-element.9, f32[640]{0:T(1024)S(1)} %get-tuple-element.8, f32[]{:T(128)} %bitcast.99), channel_id=1, replica_groups=mesh['dp'=8,'rows'=4] {'dp','rows'}, use_global_device_ids=true, to_apply=%region_18.19 | all-reduce | flops 1281 | bytes 10248 | tf_op jit(solution)/shard_map/psum | solution.py:186
  366.2 2.9 copy.48
  (159 shorter events, 56.9 us)
Async XLA Ops:
  7.2 28.6 %copy-start.9 = (bf16[1,8,16,640]{3,2,1,0:T(8,128)(2,1)S(1)}, bf16[1,8,16,640]{3,2,1,0:T(8,128)(2,1)}, u32[]{:S(2)}) copy-start(bf16[1,8,16,640]{3,2,1,0:T(8,128)(2,1)} %param.10) | copy-start | bytes 491524
  7.2 28.6 %copy-start.6 = (bf16[1,8,16,640]{3,2,1,0:T(8,128)(2,1)S(1)}, bf16[1,8,16,640]{3,2,1,0:T(8,128)(2,1)}, u32[]{:S(2)}) copy-start(bf16[1,8,16,640]{3,2,1,0:T(8,128)(2,1)} %param.11) | copy-start | bytes 491524
  7.2 28.6 %copy-start.24 = (f32[640]{0:T(1024)S(1)}, f32[640]{0:T(1024)}, u32[]{:S(2)}) copy-start(f32[640]{0:T(1024)} %param.15) | copy-start | bytes 7684
  7.2 28.6 %copy-start.22 = (f32[640]{0:T(1024)S(1)}, f32[640]{0:T(1024)}, u32[]{:S(2)}) copy-start(f32[640]{0:T(1024)} %param.16) | copy-start | bytes 7684
  7.2 118.0 %all-gather.3.cloned.1.call-start = ((), (), s32[]{:S(2)}) async-start(), calls=%async_computation.1 | async-start | bytes 8294400 | tf_op jit(solution)/shard_map/all_gather | solution.py:153
  7.9 229.3 %all-gather.5.cloned.1.call-start = ((), (), s32[]{:S(2)}) async-start(), calls=%async_computation.2 | async-start | bytes 8294400 | tf_op jit(solution)/shard_map/all_gather | solution.py:154
  26.2 21.4 %copy-start.14 = (f32[640]{0:T(1024)}, f32[640]{0:T(1024)S(1)}, u32[]{:S(2)}) copy-start(f32[640]{0:T(1024)S(1)} %sub.73) | copy-start | bytes 7684
  37.4 24.1 %copy-start.4 = (bf16[1,8,16,640]{3,2,1,0:T(8,128)(2,1)}, bf16[1,8,16,640]{3,2,1,0:T(8,128)(2,1)S(1)}, u32[]{:S(2)}) copy-start(bf16[1,8,16,640]{3,2,1,0:T(8,128)(2,1)S(1)} %get-tuple-element.28) | copy-start | bytes 491524
  37.4 2.7 collective-permute-start
  38.8 3.6 collective-permute-start.1
  47.6 14.7 %all-to-all-start = ((bf16[8,2,7200]{2,1,0:T(2,128)(2,1)}), bf16[8,2,7200]{2,1,0:T(2,128)(2,1)S(1)}, u32[]{:S(2)}, u32[]{:S(2)}) async-start(bf16[8,2,7200]{2,1,0:T(2,128)(2,1)} %reshape.527), calls=%async_computation | async-start | bytes 466944 | tf_op jit(solution)/shard_map/all_to_all | solution.py:166
  53.7 312.5 %all-reduce.8.cloned.1.call-start = ((), (), s32[]{:S(2)}) async-start(), calls=%async_computation.3 | async-start | bytes 3686400 | tf_op jit(solution)/shard_map/psum | solution.py:169
  53.8 7.3 %collective-permute-start.2 = (bf16[1,1,16,640]{3,2,1,0:T(8,128)(2,1)S(1)}, bf16[1,1,16,640]{3,2,1,0:T(8,128)(2,1)S(1)}, u32[]{:S(2)}, u32[]{:S(2)}) collective-permute-start(bf16[1,1,16,640]{3,2,1,0:T(8,128)(2,1)S(1)} %get-tuple-element.34), channel_id=1, source_target_pairs={{0,1},{1,2},{2,3},{4,5},{5,6},{6,7},{8,9},{9,10},{10,11},{12,13},{... | collective-permute-start | bytes 61448 | tf_op jit(solution)/shard_map/ppermute | solution.py:43
  58.3 3.1 collective-permute-start.3
  127.4 122.1 %slice-start = ((s8[7372800]{0:T(1024)(128)(4,1)}), s8[3178496]{0:T(1024)(128)(4,1)S(1)}, s32[]{:S(2)}) async-start(s8[7372800]{0:T(1024)(128)(4,1)} %bitcast.255), calls=%async_computation.4 | async-start | bytes 6356992
  255.4 8.0 %collective-permute-start.4 = (bf16[1,8,16,640]{3,2,1,0:T(8,128)(2,1)S(1)}, bf16[1,8,16,640]{3,2,1,0:T(8,128)(2,1)S(1)}, u32[]{:S(2)}, u32[]{:S(2)}) collective-permute-start(bf16[1,8,16,640]{3,2,1,0:T(8,128)(2,1)S(1)} %get-tuple-element.31), channel_id=1, source_target_pairs={{0,4},{4,8},{8,12},{12,16},{16,20},{20,24},{24,28},{28,0},{1,5},{5... | collective-permute-start | bytes 491528 | tf_op jit(solution)/shard_map/ppermute | solution.py:27
  256.6 11.2 %collective-permute-start.11 = (bf16[1,1,16,640]{3,2,1,0:T(8,128)(2,1)}, bf16[1,1,16,640]{3,2,1,0:T(8,128)(2,1)S(1)}, u32[]{:S(2)}, u32[]{:S(2)}) collective-permute-start(bf16[1,1,16,640]{3,2,1,0:T(8,128)(2,1)} %get-tuple-element.32), channel_id=1, source_target_pairs={{0,1},{1,2},{2,3},{4,5},{5,6},{6,7},{8,9},{9,10},{10,11},{12,13},{... | collective-permute-start | bytes 61448 | tf_op jit(solution)/shard_map/ppermute | solution.py:43
  257.9 10.5 %collective-permute-start.12 = (bf16[1,1,16,640]{3,2,1,0:T(8,128)(2,1)S(1)}, bf16[1,1,16,640]{3,2,1,0:T(8,128)(2,1)S(1)}, u32[]{:S(2)}, u32[]{:S(2)}) collective-permute-start(bf16[1,1,16,640]{3,2,1,0:T(8,128)(2,1)S(1)} %get-tuple-element.33), channel_id=1, source_target_pairs={{1,0},{2,1},{3,2},{5,4},{6,5},{7,6},{9,8},{10,9},{11,10},{13,12},{... | collective-permute-start | bytes 61448 | tf_op jit(solution)/shard_map/ppermute | solution.py:46
  263.4 8.1 %collective-permute-start.5 = (bf16[1,8,16,640]{3,2,1,0:T(8,128)(2,1)S(1)}, bf16[1,8,16,640]{3,2,1,0:T(8,128)(2,1)}, u32[]{:S(2)}, u32[]{:S(2)}) collective-permute-start(bf16[1,8,16,640]{3,2,1,0:T(8,128)(2,1)S(1)} %collective-permute-done.4), channel_id=1, source_target_pairs={{0,4},{4,8},{8,12},{12,16},{16,20},{20,24},{24,28},{28,0},{1,5},{5... | collective-permute-start | bytes 491528 | tf_op jit(solution)/shard_map/ppermute | solution.py:27
  271.6 8.2 %collective-permute-start.6 = (bf16[1,8,16,640]{3,2,1,0:T(8,128)(2,1)}, bf16[1,8,16,640]{3,2,1,0:T(8,128)(2,1)S(1)}, u32[]{:S(2)}, u32[]{:S(2)}) collective-permute-start(bf16[1,8,16,640]{3,2,1,0:T(8,128)(2,1)} %collective-permute-done.5), channel_id=1, source_target_pairs={{0,4},{4,8},{8,12},{12,16},{16,20},{20,24},{24,28},{28,0},{1,5},{5... | collective-permute-start | bytes 491528 | tf_op jit(solution)/shard_map/ppermute | solution.py:27
  279.8 8.0 %collective-permute-start.7 = (bf16[1,8,16,640]{3,2,1,0:T(8,128)(2,1)S(1)}, bf16[1,8,16,640]{3,2,1,0:T(8,128)(2,1)S(1)}, u32[]{:S(2)}, u32[]{:S(2)}) collective-permute-start(bf16[1,8,16,640]{3,2,1,0:T(8,128)(2,1)S(1)} %collective-permute-done.6), channel_id=1, source_target_pairs={{0,4},{4,8},{8,12},{12,16},{16,20},{20,24},{24,28},{28,0},{1,5},{5... | collective-permute-start | bytes 491528 | tf_op jit(solution)/shard_map/ppermute | solution.py:27
  287.8 8.7 %collective-permute-start.8 = (bf16[1,8,16,640]{3,2,1,0:T(8,128)(2,1)S(1)}, bf16[1,8,16,640]{3,2,1,0:T(8,128)(2,1)S(1)}, u32[]{:S(2)}, u32[]{:S(2)}) collective-permute-start(bf16[1,8,16,640]{3,2,1,0:T(8,128)(2,1)S(1)} %collective-permute-done.7), channel_id=1, source_target_pairs={{0,4},{4,8},{8,12},{12,16},{16,20},{20,24},{24,28},{28,0},{1,5},{5... | collective-permute-start | bytes 491528 | tf_op jit(solution)/shard_map/ppermute | solution.py:27
  296.5 9.7 %collective-permute-start.9 = (bf16[1,8,16,640]{3,2,1,0:T(8,128)(2,1)S(1)}, bf16[1,8,16,640]{3,2,1,0:T(8,128)(2,1)S(1)}, u32[]{:S(2)}, u32[]{:S(2)}) collective-permute-start(bf16[1,8,16,640]{3,2,1,0:T(8,128)(2,1)S(1)} %collective-permute-done.8), channel_id=1, source_target_pairs={{0,4},{4,8},{8,12},{12,16},{16,20},{20,24},{24,28},{28,0},{1,5},{5... | collective-permute-start | bytes 491528 | tf_op jit(solution)/shard_map/ppermute | solution.py:27
  306.2 8.0 %collective-permute-start.10 = (bf16[1,8,16,640]{3,2,1,0:T(8,128)(2,1)S(1)}, bf16[1,8,16,640]{3,2,1,0:T(8,128)(2,1)S(1)}, u32[]{:S(2)}, u32[]{:S(2)}) collective-permute-start(bf16[1,8,16,640]{3,2,1,0:T(8,128)(2,1)S(1)} %collective-permute-done.9), channel_id=1, source_target_pairs={{0,4},{4,8},{8,12},{12,16},{16,20},{20,24},{24,28},{28,0},{1,5},{5... | collective-permute-start | bytes 491528 | tf_op jit(solution)/shard_map/ppermute | solution.py:27
  (21 other events, 98.1 us)
Sparse Core Ops, SparseCore 0:
  10.3 114.9 all-gather.2
  127.5 109.7 all-gather.4
  319.3 46.9 all-reduce.7
